TPU v7x, 32 devices: a whole 2x2x4 slice. The times are simulated.
32 devices in a mesh: frame: 4 (over y, x), row: 8 (over z, core).
Axes of the slice: x: 2, y: 2, z: 4, core: 2. Of those that a mesh axis runs over, the one named last changes fastest.
Arguments:
- residual_in: bfloat16 [4, 8, 64, 768], P('frame', 'row'), may hold values from -6 to 6
- q_spatial: bfloat16 [4, 8, 64, 768], P('frame', 'row'), may hold values from -250 to 250
- k_spatial: bfloat16 [4, 8, 64, 768], P('frame', 'row'), may hold values from -250 to 250
- v_spatial: bfloat16 [4, 8, 64, 768], P('frame', 'row'), may hold values from -6 to 6
- q_temporal: bfloat16 [4, 8, 64, 768], P('frame', 'row'), may hold values from -250 to 250
- k_temporal: bfloat16 [4, 8, 64, 768], P('frame', 'row'), may hold values from -250 to 250
- conv_weight: float32 [3, 3, 768], replicated, may hold values from -2 to 2
- conv_bias: float32 [768], replicated, may hold values from -3 to 3
Outputs:
- spatial_out: bfloat16 [4, 8, 64, 768], P('frame', 'row')
- block_out: bfloat16 [4, 8, 64, 768], P('frame', 'row')
All inputs are finite; a program needn't handle non-finite values.
Results may differ from a plain program's by a relative error of at most 0.0061.
Values may be sent and summed in bfloat16 or wider, within the bound.
A program may use at most 64 MiB of HBM per device.

v0:
```python
import math
import jax
import jax.numpy as jnp
from jax import lax
from jax.sharding import PartitionSpec as P

HEADS = 12
HEAD_DIM = 64


def padded(block, sides, width):
    for axis, dim in sides:
        count = lax.axis_size(axis)
        forward = [(i, i + 1) for i in range(count - 1)]
        backward = [(target, source) for source, target in forward]
        low = lax.ppermute(
            lax.slice_in_dim(block, block.shape[dim] - width, None, axis=dim), axis, forward
        )
        high = lax.ppermute(lax.slice_in_dim(block, 0, width, axis=dim), axis, backward)
        block = jnp.concatenate([low, block, high], axis=dim)
    return block


def absorb(carry_state, query_heads, key_rows, value_rows):
    running_max, running_sum, weighted = carry_state
    scores = jnp.einsum(
        "thd,khd->htk", query_heads, key_rows, preferred_element_type=jnp.float32
    ) * HEAD_DIM ** (-0.5)
    new_max = jnp.maximum(running_max, jnp.max(scores, axis=-1))
    shrink = jnp.exp(running_max - new_max)
    raised = jnp.exp(scores - new_max[..., None])
    running_sum = running_sum * shrink + jnp.sum(raised, axis=-1)
    weighted = weighted * shrink[..., None] + jnp.einsum(
        "htk,khd->htd", raised.astype(jnp.bfloat16), value_rows, preferred_element_type=jnp.float32
    )
    return (new_max, running_sum, weighted)


def frame_attention(queries, keys, values):
    frames, rows_here, across, channels = queries.shape
    shape5 = (frames, rows_here, across, HEADS, HEAD_DIM)
    scores = jnp.einsum(
        "fywhd,gywhd->ywhfg",
        queries.reshape(shape5),
        keys.reshape(shape5),
        preferred_element_type=jnp.float32,
    ) * HEAD_DIM ** (-0.5)
    frame_ids = jnp.arange(frames)
    allowed = frame_ids[:, None] >= frame_ids[None, :]
    scores = jnp.where(allowed, scores, -1e30)
    peak = jnp.max(scores, axis=-1, keepdims=True)
    raised = jnp.exp(scores - peak)
    totals = jnp.sum(raised, axis=-1)
    blended = jnp.einsum(
        "ywhfg,gywhd->fywhd",
        raised.astype(jnp.bfloat16),
        values.reshape(shape5),
        preferred_element_type=jnp.float32,
    )
    blended = blended / jnp.moveaxis(totals, 3, 0)[..., None]
    return blended.reshape(frames, rows_here, across, channels).astype(jnp.bfloat16)


def attend_frames(triple):
    return frame_attention(triple[0], triple[1], triple[2])


def on_device(
    residual_in, q_spatial, k_spatial, v_spatial, q_temporal, k_temporal, conv_weight, conv_bias
):
    rows_here = q_spatial.shape[1]
    across = q_spatial.shape[2]
    tokens_here = rows_here * across
    query_heads = q_spatial.reshape(tokens_here, HEADS, HEAD_DIM)
    start_state = (
        jnp.full((HEADS, tokens_here), -1e30, jnp.float32),
        jnp.zeros((HEADS, tokens_here), jnp.float32),
        jnp.zeros((HEADS, tokens_here, HEAD_DIM), jnp.float32),
    )
    carry_state = start_state
    key_rows = lax.all_gather(k_spatial, "row", axis=1, tiled=True).reshape(-1, HEADS, HEAD_DIM)
    value_rows = lax.all_gather(v_spatial, "row", axis=1, tiled=True).reshape(-1, HEADS, HEAD_DIM)
    length = key_rows.shape[0]
    block = math.gcd(length, 512)
    for begin in range(0, length, block):
        carry_state = absorb(
            carry_state,
            query_heads,
            key_rows[begin : begin + block],
            value_rows[begin : begin + block],
        )
    running_max, running_sum, weighted = carry_state
    attended = weighted / running_sum[..., None]
    spatial_out = jnp.transpose(attended, (1, 0, 2)).reshape(q_spatial.shape).astype(jnp.bfloat16)
    hidden = (residual_in.astype(jnp.float32) + spatial_out.astype(jnp.float32)).astype(
        jnp.bfloat16
    )
    temporal = attend_frames(
        (
            lax.all_to_all(q_temporal, "frame", split_axis=2, concat_axis=0, tiled=True),
            lax.all_to_all(k_temporal, "frame", split_axis=2, concat_axis=0, tiled=True),
            lax.all_to_all(hidden, "frame", split_axis=2, concat_axis=0, tiled=True),
        )
    )
    returned = lax.all_to_all(temporal, "frame", split_axis=0, concat_axis=2, tiled=True)
    mixed = (hidden.astype(jnp.float32) + returned.astype(jnp.float32)).astype(jnp.bfloat16)
    extended = padded(mixed, (("row", 1),), 1)
    widened = jnp.pad(extended, ((0, 0), (0, 0), (1, 1), (0, 0))).astype(jnp.float32)
    conv = jnp.zeros(mixed.shape, jnp.float32) + conv_bias
    for first in range(3):
        for second in range(3):
            conv = (
                conv
                + conv_weight[first, second]
                * widened[:, first : first + rows_here, second : second + across]
            )
    block_out = (mixed.astype(jnp.float32) + jax.nn.gelu(conv)).astype(jnp.bfloat16)
    return (spatial_out, block_out)


def solution(mesh):
    placed = (
        P("frame", "row", None, None),
        P("frame", "row", None, None),
        P("frame", "row", None, None),
        P("frame", "row", None, None),
        P("frame", "row", None, None),
        P("frame", "row", None, None),
        P(),
        P(),
    )
    return jax.shard_map(
        on_device,
        mesh=mesh,
        in_specs=placed,
        out_specs=(P("frame", "row", None, None), P("frame", "row", None, None)),
        check_vma=False,
    )
```

profile of v0, /device:TPU:1, one launch (start us, length us, event | category | flops | bytes accessed | tf_op | source)
XLA Modules:
  0.0 86.6 jit_solution(11516909779274011631)
XLA Ops:
  0.6 1.0 %copy.56 = bf16[1,1,64,768]{3,1,0,2:T(2,128)(2,1)S(1)} copy(bf16[1,1,64,768]{3,2,1,0:T(8,128)(2,1)} %param.13) | data formatting | bytes 196608 | tf_op args[5]
  1.7 0.5 broadcast.79
  2.2 1.1 %reduce.28 = bf16[64,768]{1,0:T(8,128)(2,1)S(1)} reduce(bf16[64,1,1,768]{3,2,1,0:T(2,128)(2,1)S(1)} %bitcast.61, bf16[]{:T(256)} %broadcast.79), dimensions={1,2}, to_apply=%bitcast.58.reduce_sub_computation | reduce | bytes 196610
  3.3 0.7 reshape.173
  4.0 4.3 %all-to-all-start.2 = ((bf16[4,2,6144]{2,1,0:T(2,128)(2,1)}), bf16[4,2,6144]{2,1,0:T(2,128)(2,1)S(1)}, u32[]{:S(2)}, u32[]{:S(2)}) async-start(bf16[4,2,6144]{2,1,0:T(2,128)(2,1)} %reshape.173), calls=%async_computation.2 | async-start | bytes 196608 | tf_op jit(solution)/shard_map/all_to_all | solution.py:101
  8.2 16.7 %all_gather.7 = bf16[1,8,64,768]{3,2,0,1:T(8,128)(2,1)S(1)} all-gather(bf16[1,1,64,768]{3,2,0,1:T(8,128)(2,1)} %bitcast.67), channel_id=1, replica_groups=mesh['frame'=4,'row'=8] {'row'}, dimensions={1}, use_global_device_ids=true | all-gather | bytes 884736 | tf_op jit(solution)/shard_map/all_gather | solution.py:82
  25.0 1.1 %copy.27 = bf16[1,8,64,768]{2,1,3,0:T(8,128)(2,1)S(1)} copy(bf16[1,8,64,768]{3,2,0,1:T(8,128)(2,1)S(1)} %all_gather.7) | data formatting | bytes 1572864 | tf_op jit(solution)/shard_map/all_gather | solution.py:82
  26.1 0.0 copy-start.1
  26.1 1.0 %reshape.156 = bf16[512,12,64]{0,2,1:T(8,128)(2,1)S(1)} reshape(bf16[1,8,64,768]{2,1,3,0:T(8,128)(2,1)S(1)} %copy.27) | data formatting | bytes 1572864 | tf_op jit(solution)/shard_map/reshape | solution.py:82
  27.1 0.0 copy-done.1
  27.1 15.7 %all_gather.6 = bf16[1,8,64,768]{3,2,0,1:T(8,128)(2,1)S(1)} all-gather(bf16[1,1,64,768]{3,2,0,1:T(8,128)(2,1)S(1)} %bitcast.68), channel_id=1, replica_groups=mesh['frame'=4,'row'=8] {'row'}, dimensions={1}, use_global_device_ids=true | all-gather | bytes 884736 | tf_op jit(solution)/shard_map/all_gather | solution.py:81
  42.8 1.1 %copy.24 = bf16[1,8,64,768]{2,1,3,0:T(8,128)(2,1)S(1)} copy(bf16[1,8,64,768]{3,2,0,1:T(8,128)(2,1)S(1)} %all_gather.6) | data formatting | bytes 1572864 | tf_op jit(solution)/shard_map/all_gather | solution.py:81
  43.9 0.0 copy-start.2
  44.0 1.0 %reshape.155 = bf16[512,12,64]{0,2,1:T(8,128)(2,1)S(1)} reshape(bf16[1,8,64,768]{2,1,3,0:T(8,128)(2,1)S(1)} %copy.24) | data formatting | bytes 1572864 | tf_op jit(solution)/shard_map/reshape | solution.py:81
  44.9 0.0 copy-done.2
  44.9 0.2 reshape.154
  45.1 0.4 fusion.44
  45.6 0.6 fusion
  46.1 0.0 copy-start.3
  46.2 0.5 fusion.5
  46.7 0.0 copy-start.4
  46.7 0.1 copy.28
  46.9 0.2 convert_element_type.89
  47.0 0.0 copy-done.3
  47.0 0.0 copy-start
  47.1 0.2 copy.57
  47.2 1.1 %reduce.29 = bf16[64,768]{1,0:T(8,128)(2,1)S(1)} reduce(bf16[64,1,1,768]{3,2,1,0:T(2,128)(2,1)S(1)} %bitcast.63, bf16[]{:T(256)} %broadcast.79), dimensions={1,2}, to_apply=%bitcast.59.reduce_sub_computation | reduce | bytes 196610
  48.3 0.6 reshape.175
  49.0 0.0 copy-done.4
  49.0 0.2 copy.58
  49.2 1.1 %reduce.30 = bf16[64,768]{1,0:T(8,128)(2,1)S(1)} reduce(bf16[64,1,1,768]{3,2,1,0:T(2,128)(2,1)S(1)} %bitcast.62, bf16[]{:T(256)} %broadcast.79), dimensions={1,2}, to_apply=%bitcast.60.reduce_sub_computation | reduce | bytes 196610
  50.3 0.7 reshape.177
  51.0 0.0 all-to-all-done.2
  51.0 3.9 %all-to-all-start.1 = ((bf16[4,2,6144]{2,1,0:T(2,128)(2,1)}), bf16[4,2,6144]{2,1,0:T(2,128)(2,1)S(1)}, u32[]{:S(2)}, u32[]{:S(2)}) async-start(bf16[4,2,6144]{2,1,0:T(2,128)(2,1)} %reshape.175), calls=%async_computation.1 | async-start | bytes 196608 | tf_op jit(solution)/shard_map/all_to_all | solution.py:100
  54.9 0.1 reshape.174
  55.0 0.5 bitcast_reduce_fusion.2
  55.5 0.2 reshape.159
  55.7 3.0 %all-to-all-done.1 = bf16[4,2,6144]{2,1,0:T(2,128)(2,1)S(1)} async-done(((bf16[4,2,6144]{2,1,0:T(2,128)(2,1)}), bf16[4,2,6144]{2,1,0:T(2,128)(2,1)S(1)}, u32[]{:S(2)}, u32[]{:S(2)}) %all-to-all-start.1) | async-done | bytes 98336 | tf_op jit(solution)/shard_map/all_to_all | solution.py:100
  58.7 0.0 copy-done
  58.7 3.3 %all-to-all-start = ((bf16[4,2,6144]{2,1,0:T(2,128)(2,1)}), bf16[4,2,6144]{2,1,0:T(2,128)(2,1)S(1)}, u32[]{:S(2)}, u32[]{:S(2)}) async-start(bf16[4,2,6144]{2,1,0:T(2,128)(2,1)} %reshape.177), calls=%async_computation | async-start | bytes 196608 | tf_op jit(solution)/shard_map/all_to_all | solution.py:102
  62.0 0.1 reshape.176
  62.1 0.5 bitcast_reduce_fusion.1
  62.6 0.2 reshape.158
  62.8 2.9 %all-to-all-done = bf16[4,2,6144]{2,1,0:T(2,128)(2,1)S(1)} async-done(((bf16[4,2,6144]{2,1,0:T(2,128)(2,1)}), bf16[4,2,6144]{2,1,0:T(2,128)(2,1)S(1)}, u32[]{:S(2)}, u32[]{:S(2)}) %all-to-all-start) | async-done | bytes 98336 | tf_op jit(solution)/shard_map/all_to_all | solution.py:102
  65.7 0.1 reshape.178
  65.8 0.5 bitcast_reduce_fusion
  66.4 0.2 reshape.157
  66.6 0.5 fusion.45
  67.1 0.3 fusion.17
  67.4 0.0 copy-start.5
  67.5 0.5 fusion.7
  68.0 0.0 copy-start.6
  68.0 0.2 convert_element_type.96
  68.2 6.2 %all_to_all.16 = bf16[4,1,16,768]{3,2,1,0:T(8,128)(2,1)S(1)} all-to-all(bf16[4,1,16,768]{3,2,1,0:T(8,128)(2,1)S(1)} %bitcast.65), channel_id=1, replica_groups=mesh['frame'=4,'row'=8] {'frame'}, dimensions={0} | all-to-all | bytes 196608 | tf_op jit(solution)/shard_map/all_to_all | solution.py:105
  74.4 5.8 %collective-permute-start.1 = (bf16[1,1,64,768]{3,2,1,0:T(8,128)(2,1)S(1)}, bf16[1,1,64,768]{3,2,1,0:T(8,128)(2,1)S(1)}, u32[]{:S(2)}, u32[]{:S(2)}) collective-permute-start(bf16[1,1,64,768]{3,2,1,0:T(8,128)(2,1)S(1)} %fusion.38), channel_id=1, source_target_pairs={{1,0},{2,1},{3,2},{4,3},{5,4},{6,5},{7,6},{9,8},{10,9},{11,10},{12... | collective-permute-start | bytes 294920 | tf_op jit(solution)/shard_map/ppermute | solution.py:19
  80.2 3.8 %collective-permute-start = (bf16[1,1,64,768]{3,2,1,0:T(8,128)(2,1)S(1)}, bf16[1,1,64,768]{3,2,1,0:T(8,128)(2,1)S(1)}, u32[]{:S(2)}, u32[]{:S(2)}) collective-permute-start(bf16[1,1,64,768]{3,2,1,0:T(8,128)(2,1)S(1)} %fusion.38), channel_id=1, source_target_pairs={{0,1},{1,2},{2,3},{3,4},{4,5},{5,6},{6,7},{8,9},{9,10},{10,11},{11... | collective-permute-start | bytes 294920 | tf_op jit(solution)/shard_map/ppermute | solution.py:16
  84.0 0.0 copy-done.5
  84.0 0.1 slice_reduce_fusion.8
  84.1 0.3 collective-permute-done.1
  84.3 1.3 %collective-permute-done = bf16[1,1,64,768]{3,2,1,0:T(8,128)(2,1)S(1)} collective-permute-done((bf16[1,1,64,768]{3,2,1,0:T(8,128)(2,1)S(1)}, bf16[1,1,64,768]{3,2,1,0:T(8,128)(2,1)S(1)}, u32[]{:S(2)}, u32[]{:S(2)}) %collective-permute-start) | collective-permute-done | bytes 98336 | tf_op jit(solution)/shard_map/ppermute | solution.py:16
  85.6 0.1 fusion.16
  85.7 0.0 copy-done.6
  85.7 0.9 %fusion.27 = bf16[1,1,64,768]{3,2,1,0:T(8,128)(2,1)} fusion(f32[1,3,66,768]{3,2,1,0:T(8,128)S(1)} %fusion.16, bf16[1,1,64,768]{3,2,1,0:T(8,128)(2,1)S(1)} %fusion.38, f32[768]{0:T(1024)S(1)} %get-tuple-element.9, f32[768]{0:T(1024)S(1)} %get-tuple-element.10, f32[768]{0:T(1024)S(1)} %get-tuple-element.3, f32[768]{0:T(1024)S(1)} %get-tuple-element.4, ...), kind=kLoop, calls=%fused_computation.35 | loop fusion | flops 1425408 | bytes 1996800 | tf_op jit(solution)/shard_map/convert_element_type | solution.py:117
  (6 shorter events, 0.1 us)
Async XLA Ops:
  4.0 47.0 %all-to-all-start.2 = ((bf16[4,2,6144]{2,1,0:T(2,128)(2,1)}), bf16[4,2,6144]{2,1,0:T(2,128)(2,1)S(1)}, u32[]{:S(2)}, u32[]{:S(2)}) async-start(bf16[4,2,6144]{2,1,0:T(2,128)(2,1)} %reshape.173), calls=%async_computation.2 | async-start | bytes 196608 | tf_op jit(solution)/shard_map/all_to_all | solution.py:101
  26.1 1.0 %copy-start.1 = (bf16[1,1,64,768]{3,2,1,0:T(8,128)(2,1)S(1)}, bf16[1,1,64,768]{3,2,1,0:T(8,128)(2,1)}, u32[]{:S(2)}) copy-start(bf16[1,1,64,768]{3,2,1,0:T(8,128)(2,1)} %param.10) | copy-start | bytes 294916
  43.9 1.0 %copy-start.2 = (bf16[1,1,64,768]{3,2,1,0:T(8,128)(2,1)S(1)}, bf16[1,1,64,768]{3,2,1,0:T(8,128)(2,1)}, u32[]{:S(2)}) copy-start(bf16[1,1,64,768]{3,2,1,0:T(8,128)(2,1)} %param.9) | copy-start | bytes 294916
  46.1 0.9 %copy-start.3 = (bf16[1,1,64,768]{3,2,1,0:T(8,128)(2,1)S(1)}, bf16[1,1,64,768]{3,2,1,0:T(8,128)(2,1)}, u32[]{:S(2)}) copy-start(bf16[1,1,64,768]{3,2,1,0:T(8,128)(2,1)} %param.12) | copy-start | bytes 294916
  46.7 2.3 %copy-start.4 = (bf16[1,1,64,768]{3,2,1,0:T(8,128)(2,1)S(1)}, bf16[1,1,64,768]{3,2,1,0:T(8,128)(2,1)}, u32[]{:S(2)}) copy-start(bf16[1,1,64,768]{3,2,1,0:T(8,128)(2,1)} %param.8) | copy-start | bytes 294916
  47.0 11.6 %copy-start = (bf16[1,1,64,768]{3,2,1,0:T(8,128)(2,1)}, bf16[1,1,64,768]{3,2,1,0:T(8,128)(2,1)S(1)}, u32[]{:S(2)}) copy-start(bf16[1,1,64,768]{3,2,1,0:T(8,128)(2,1)S(1)} %convert_element_type.89) | copy-start | bytes 294916
  51.0 7.7 %all-to-all-start.1 = ((bf16[4,2,6144]{2,1,0:T(2,128)(2,1)}), bf16[4,2,6144]{2,1,0:T(2,128)(2,1)S(1)}, u32[]{:S(2)}, u32[]{:S(2)}) async-start(bf16[4,2,6144]{2,1,0:T(2,128)(2,1)} %reshape.175), calls=%async_computation.1 | async-start | bytes 196608 | tf_op jit(solution)/shard_map/all_to_all | solution.py:100
  58.7 7.1 %all-to-all-start = ((bf16[4,2,6144]{2,1,0:T(2,128)(2,1)}), bf16[4,2,6144]{2,1,0:T(2,128)(2,1)S(1)}, u32[]{:S(2)}, u32[]{:S(2)}) async-start(bf16[4,2,6144]{2,1,0:T(2,128)(2,1)} %reshape.177), calls=%async_computation | async-start | bytes 196608 | tf_op jit(solution)/shard_map/all_to_all | solution.py:102
  67.4 16.5 %copy-start.5 = (f32[3,3,768]{2,1,0:T(4,128)S(1)}, f32[3,3,768]{2,1,0:T(4,128)}, u32[]{:S(2)}) copy-start(f32[3,3,768]{2,1,0:T(4,128)} %param.14) | copy-start | bytes 82948
  68.0 17.7 %copy-start.6 = (f32[768]{0:T(1024)S(1)}, f32[768]{0:T(1024)}, u32[]{:S(2)}) copy-start(f32[768]{0:T(1024)} %param.15) | copy-start | bytes 9220
  74.4 9.9 %collective-permute-start.1 = (bf16[1,1,64,768]{3,2,1,0:T(8,128)(2,1)S(1)}, bf16[1,1,64,768]{3,2,1,0:T(8,128)(2,1)S(1)}, u32[]{:S(2)}, u32[]{:S(2)}) collective-permute-start(bf16[1,1,64,768]{3,2,1,0:T(8,128)(2,1)S(1)} %fusion.38), channel_id=1, source_target_pairs={{1,0},{2,1},{3,2},{4,3},{5,4},{6,5},{7,6},{9,8},{10,9},{11,10},{12... | collective-permute-start | bytes 294920 | tf_op jit(solution)/shard_map/ppermute | solution.py:19
  80.2 5.4 %collective-permute-start = (bf16[1,1,64,768]{3,2,1,0:T(8,128)(2,1)S(1)}, bf16[1,1,64,768]{3,2,1,0:T(8,128)(2,1)S(1)}, u32[]{:S(2)}, u32[]{:S(2)}) collective-permute-start(bf16[1,1,64,768]{3,2,1,0:T(8,128)(2,1)S(1)} %fusion.38), channel_id=1, source_target_pairs={{0,1},{1,2},{2,3},{3,4},{4,5},{5,6},{6,7},{8,9},{9,10},{10,11},{11... | collective-permute-start | bytes 294920 | tf_op jit(solution)/shard_map/ppermute | solution.py:16
where the time goes:
time: 87.2 us; the launch traced here: 86.6 us
  blocking collectives  38.6 us (44%)
  starting transfers between devices  21 us (24%)
  local copies, waits for them, and re-layouts  11.2 us (13%)
  waiting for transfers between devices  7.45 us (9%)
  other arithmetic  5.33 us (6%)
  matrix products  2.02 us (2%)
  between operations  0.96 us (1%)
    all_gather x1, blocking collectives, on_device(): lax.all_gather(v_spatial, 'row', axis=1, tiled=True)  16.7 us
    all_gather x1, blocking collectives, on_device(): lax.all_gather(k_spatial, 'row', axis=1, tiled=True)  15.7 us
    all_to_all x1, blocking collectives, on_device(): lax.all_to_all(temporal, 'frame', split_axis=0, concat_axis=2, tiled=True)  6.16 us
    ppermute x1, starting transfers between devices, padded(): lax.ppermute(lax.slice_in_dim(block, 0, width, axis=dim), axis, backward)  5.79 us
    all_to_all x1, starting transfers between devices, on_device(): lax.all_to_all(k_temporal, 'frame', split_axis=2, concat_axis=0, tiled=True)  4.25 us
    unnamed x23, local copies, waits for them, and re-layouts  4.01 us
    all_to_all x1, starting transfers between devices, on_device(): lax.all_to_all(q_temporal, 'frame', split_axis=2, concat_axis=0, tiled=True)  3.9 us
    ppermute x1, starting transfers between devices, padded(): lax.ppermute(lax.slice_in_dim(block, block.shape[dim] - width, None, axis...  3.78 us
  transfers between devices with their start and end apart: 5, of which 4 were waited for; matrix products, arithmetic and copies ran while one was open for 14% of the time, Pallas kernels for 0%

commit v1 on v0

--- a/solution.py
+++ b/solution.py
@@ -97,7 +97,12 @@
     )
     temporal = attend_frames(
         (
-            lax.all_to_all(q_temporal, "frame", split_axis=2, concat_axis=0, tiled=True),
+            jnp.concatenate(
+                lax.all_to_all(
+                    jnp.stack(jnp.split(q_temporal, lax.axis_size("frame"), axis=2)), "frame", 0, 0
+                ),
+                axis=0,
+            ),
             lax.all_to_all(k_temporal, "frame", split_axis=2, concat_axis=0, tiled=True),
             lax.all_to_all(hidden, "frame", split_axis=2, concat_axis=0, tiled=True),
         )

time: 87.2 us -> 85.7 us (0.983)
  local copies, waits for them, and re-layouts: 11.2 us -> 9.89 us
    unnamed x3 -> x2, other arithmetic: 3.35 us -> 2.49 us
    unnamed x23 -> x20, local copies, waits for them, and re-layouts: 4.01 us -> 3.23 us
  transfers between devices with their start and end apart: 5 -> 5, of which waited for: 4 -> 4; matrix products, arithmetic and copies ran while one was open for 14% -> 12% of each run, Pallas kernels for 0% -> 0%
where the time goes in v1:
time: 85.7 us; the launch traced here: 85.1 us
  blocking collectives  38.6 us (45%)
  starting transfers between devices  21 us (25%)
  local copies, waits for them, and re-layouts  9.89 us (12%)
  waiting for transfers between devices  7.45 us (9%)
  other arithmetic  5.11 us (6%)
  matrix products  2.01 us (2%)
  between operations  0.95 us (1%)
    all_gather x1, blocking collectives, on_device(): lax.all_gather(v_spatial, 'row', axis=1, tiled=True)  16.7 us
    all_gather x1, blocking collectives, on_device(): lax.all_gather(k_spatial, 'row', axis=1, tiled=True)  15.7 us
    all_to_all x1, blocking collectives, on_device(): lax.all_to_all(temporal, 'frame', split_axis=0, concat_axis=2, tiled=True)  6.16 us
    ppermute x1, starting transfers between devices, padded(): lax.ppermute(lax.slice_in_dim(block, 0, width, axis=dim), axis, backward)  5.77 us
    all_to_all x1, starting transfers between devices, on_device(): lax.all_to_all(k_temporal, 'frame', split_axis=2, concat_axis=0, tiled=True)  4.25 us
    all_to_all x1, starting transfers between devices, on_device(): lax.all_to_all(hidden, 'frame', split_axis=2, concat_axis=0, tiled=True)  3.91 us
    ppermute x1, starting transfers between devices, padded(): lax.ppermute(lax.slice_in_dim(block, block.shape[dim] - width, None, axis...  3.78 us
    all_to_all x1, starting transfers between devices, on_device(): lax.all_to_all(jnp.stack(jnp.split(q_temporal, lax.axis_size('frame'), ax...  3.3 us
  transfers between devices with their start and end apart: 5, of which 4 were waited for; matrix products, arithmetic and copies ran while one was open for 12% of the time, Pallas kernels for 0%

profile of v1, /device:TPU:1, one launch (start us, length us, event | category | flops | bytes accessed | tf_op | source)
XLA Modules:
  0.0 85.1 jit_solution(13488533746869792194)
XLA Ops:
  0.6 1.0 %copy.54 = bf16[1,1,64,768]{3,1,0,2:T(2,128)(2,1)S(1)} copy(bf16[1,1,64,768]{3,2,1,0:T(8,128)(2,1)} %param.13) | data formatting | bytes 196608 | tf_op args[5]
  1.7 0.6 broadcast.78
  2.3 1.2 %reduce.26 = bf16[64,768]{1,0:T(8,128)(2,1)S(1)} reduce(bf16[64,1,1,768]{3,2,1,0:T(2,128)(2,1)S(1)} %bitcast.66, bf16[]{:T(256)} %broadcast.78), dimensions={1,2}, to_apply=%bitcast.64.reduce_sub_computation | reduce | bytes 196610
  3.5 0.7 reshape.167
  4.2 4.3 %all-to-all-start.2 = ((bf16[4,2,6144]{2,1,0:T(2,128)(2,1)}), bf16[4,2,6144]{2,1,0:T(2,128)(2,1)S(1)}, u32[]{:S(2)}, u32[]{:S(2)}) async-start(bf16[4,2,6144]{2,1,0:T(2,128)(2,1)} %reshape.167), calls=%async_computation.2 | async-start | bytes 196608 | tf_op jit(solution)/shard_map/all_to_all | solution.py:106
  8.4 16.7 %all_gather.7 = bf16[1,8,64,768]{3,2,0,1:T(8,128)(2,1)S(1)} all-gather(bf16[1,1,64,768]{3,2,0,1:T(8,128)(2,1)} %bitcast.71), channel_id=1, replica_groups=mesh['frame'=4,'row'=8] {'row'}, dimensions={1}, use_global_device_ids=true | all-gather | bytes 884736 | tf_op jit(solution)/shard_map/all_gather | solution.py:82
  25.2 1.1 %copy.27 = bf16[1,8,64,768]{2,1,3,0:T(8,128)(2,1)S(1)} copy(bf16[1,8,64,768]{3,2,0,1:T(8,128)(2,1)S(1)} %all_gather.7) | data formatting | bytes 1572864 | tf_op jit(solution)/shard_map/all_gather | solution.py:82
  26.3 0.0 copy-start.1
  26.3 1.0 %reshape.151 = bf16[512,12,64]{0,2,1:T(8,128)(2,1)S(1)} reshape(bf16[1,8,64,768]{2,1,3,0:T(8,128)(2,1)S(1)} %copy.27) | data formatting | bytes 1572864 | tf_op jit(solution)/shard_map/reshape | solution.py:82
  27.3 0.0 copy-done.1
  27.3 15.7 %all_gather.6 = bf16[1,8,64,768]{3,2,0,1:T(8,128)(2,1)S(1)} all-gather(bf16[1,1,64,768]{3,2,0,1:T(8,128)(2,1)S(1)} %bitcast.72), channel_id=1, replica_groups=mesh['frame'=4,'row'=8] {'row'}, dimensions={1}, use_global_device_ids=true | all-gather | bytes 884736 | tf_op jit(solution)/shard_map/all_gather | solution.py:81
  43.0 1.1 %copy.24 = bf16[1,8,64,768]{2,1,3,0:T(8,128)(2,1)S(1)} copy(bf16[1,8,64,768]{3,2,0,1:T(8,128)(2,1)S(1)} %all_gather.6) | data formatting | bytes 1572864 | tf_op jit(solution)/shard_map/all_gather | solution.py:81
  44.2 0.0 copy-start.3
  44.2 1.0 %reshape.150 = bf16[512,12,64]{0,2,1:T(8,128)(2,1)S(1)} reshape(bf16[1,8,64,768]{2,1,3,0:T(8,128)(2,1)S(1)} %copy.24) | data formatting | bytes 1572864 | tf_op jit(solution)/shard_map/reshape | solution.py:81
  45.1 0.0 copy-done.3
  45.2 0.2 reshape.149
  45.3 0.4 fusion.44
  45.8 0.6 fusion
  46.4 0.0 copy-start.2
  46.4 0.0 copy-start.4
  46.4 0.5 fusion.5
  46.9 0.1 copy.28
  47.1 0.2 convert_element_type.89
  47.2 0.0 copy-done.2
  47.3 0.0 copy-start
  47.3 0.0 copy-done.4
  47.3 0.2 copy.55
  47.5 1.2 %reduce.27 = bf16[64,768]{1,0:T(8,128)(2,1)S(1)} reduce(bf16[64,1,1,768]{3,2,1,0:T(2,128)(2,1)S(1)} %bitcast.67, bf16[]{:T(256)} %broadcast.78), dimensions={1,2}, to_apply=%bitcast.65.reduce_sub_computation | reduce | bytes 196610
  48.8 0.7 reshape.169
  49.4 0.6 pad_maximum_fusion
  50.1 0.0 all-to-all-done.2
  50.1 3.9 %all-to-all-start = ((bf16[4,2,6144]{2,1,0:T(2,128)(2,1)}), bf16[4,2,6144]{2,1,0:T(2,128)(2,1)S(1)}, u32[]{:S(2)}, u32[]{:S(2)}) async-start(bf16[4,2,6144]{2,1,0:T(2,128)(2,1)} %reshape.169), calls=%async_computation | async-start | bytes 196608 | tf_op jit(solution)/shard_map/all_to_all | solution.py:107
  54.0 0.1 reshape.168
  54.1 0.5 bitcast_reduce_fusion.1
  54.6 0.2 reshape.154
  54.8 3.0 %all-to-all-done = bf16[4,2,6144]{2,1,0:T(2,128)(2,1)S(1)} async-done(((bf16[4,2,6144]{2,1,0:T(2,128)(2,1)}), bf16[4,2,6144]{2,1,0:T(2,128)(2,1)S(1)}, u32[]{:S(2)}, u32[]{:S(2)}) %all-to-all-start) | async-done | bytes 98336 | tf_op jit(solution)/shard_map/all_to_all | solution.py:107
  57.8 3.3 %all-to-all-start.1 = ((bf16[4,1,1,16,768]{4,3,2,1,0:T(8,128)(2,1)}), bf16[4,1,1,16,768]{4,3,2,1,0:T(8,128)(2,1)S(1)}, u32[]{:S(2)}, u32[]{:S(2)}) async-start(bf16[4,1,1,16,768]{4,3,2,1,0:T(8,128)(2,1)} %pad_maximum_fusion), calls=%async_computation.1 | async-start | bytes 196608 | tf_op jit(solution)/shard_map/all_to_all | solution.py:101
  61.1 0.1 reshape.170
  61.2 0.5 bitcast_reduce_fusion
  61.7 0.0 copy-done
  61.7 0.2 reshape.152
  61.9 2.9 %all-to-all-done.1 = bf16[4,1,1,16,768]{4,3,2,1,0:T(8,128)(2,1)S(1)} async-done(((bf16[4,1,1,16,768]{4,3,2,1,0:T(8,128)(2,1)}), bf16[4,1,1,16,768]{4,3,2,1,0:T(8,128)(2,1)S(1)}, u32[]{:S(2)}, u32[]{:S(2)}) %all-to-all-start.1) | async-done | bytes 98336 | tf_op jit(solution)/shard_map/all_to_all | solution.py:101
  64.8 0.2 reshape.153
  65.0 0.5 fusion.45
  65.5 0.3 fusion.17
  65.9 0.0 copy-start.5
  65.9 0.5 fusion.7
  66.4 0.0 copy-start.6
  66.5 0.2 convert_element_type.96
  66.7 6.2 %all_to_all.32 = bf16[4,1,16,768]{3,2,1,0:T(8,128)(2,1)S(1)} all-to-all(bf16[4,1,16,768]{3,2,1,0:T(8,128)(2,1)S(1)} %bitcast.69), channel_id=1, replica_groups=mesh['frame'=4,'row'=8] {'frame'}, dimensions={0} | all-to-all | bytes 196608 | tf_op jit(solution)/shard_map/all_to_all | solution.py:110
  72.9 5.8 %collective-permute-start.1 = (bf16[1,1,64,768]{3,2,1,0:T(8,128)(2,1)S(1)}, bf16[1,1,64,768]{3,2,1,0:T(8,128)(2,1)S(1)}, u32[]{:S(2)}, u32[]{:S(2)}) collective-permute-start(bf16[1,1,64,768]{3,2,1,0:T(8,128)(2,1)S(1)} %fusion.38), channel_id=1, source_target_pairs={{1,0},{2,1},{3,2},{4,3},{5,4},{6,5},{7,6},{9,8},{10,9},{11,10},{12... | collective-permute-start | bytes 294920 | tf_op jit(solution)/shard_map/ppermute | solution.py:19
  78.6 3.8 %collective-permute-start = (bf16[1,1,64,768]{3,2,1,0:T(8,128)(2,1)S(1)}, bf16[1,1,64,768]{3,2,1,0:T(8,128)(2,1)S(1)}, u32[]{:S(2)}, u32[]{:S(2)}) collective-permute-start(bf16[1,1,64,768]{3,2,1,0:T(8,128)(2,1)S(1)} %fusion.38), channel_id=1, source_target_pairs={{0,1},{1,2},{2,3},{3,4},{4,5},{5,6},{6,7},{8,9},{9,10},{10,11},{11... | collective-permute-start | bytes 294920 | tf_op jit(solution)/shard_map/ppermute | solution.py:16
  82.4 0.0 copy-done.5
  82.4 0.1 slice_reduce_fusion.8
  82.5 0.3 collective-permute-done.1
  82.8 1.3 %collective-permute-done = bf16[1,1,64,768]{3,2,1,0:T(8,128)(2,1)S(1)} collective-permute-done((bf16[1,1,64,768]{3,2,1,0:T(8,128)(2,1)S(1)}, bf16[1,1,64,768]{3,2,1,0:T(8,128)(2,1)S(1)}, u32[]{:S(2)}, u32[]{:S(2)}) %collective-permute-start) | collective-permute-done | bytes 98336 | tf_op jit(solution)/shard_map/ppermute | solution.py:16
  84.0 0.1 fusion.16
  84.1 0.0 copy-done.6
  84.1 0.9 %fusion.27 = bf16[1,1,64,768]{3,2,1,0:T(8,128)(2,1)} fusion(f32[1,3,66,768]{3,2,1,0:T(8,128)S(1)} %fusion.16, bf16[1,1,64,768]{3,2,1,0:T(8,128)(2,1)S(1)} %fusion.38, f32[768]{0:T(1024)S(1)} %get-tuple-element.9, f32[768]{0:T(1024)S(1)} %get-tuple-element.10, f32[768]{0:T(1024)S(1)} %get-tuple-element.3, f32[768]{0:T(1024)S(1)} %get-tuple-element.4, ...), kind=kLoop, calls=%fused_computation.35 | loop fusion | flops 1425408 | bytes 1996800 | tf_op jit(solution)/shard_map/convert_element_type | solution.py:122
  (7 shorter events, 0.1 us)
Async XLA Ops:
  4.2 45.9 %all-to-all-start.2 = ((bf16[4,2,6144]{2,1,0:T(2,128)(2,1)}), bf16[4,2,6144]{2,1,0:T(2,128)(2,1)S(1)}, u32[]{:S(2)}, u32[]{:S(2)}) async-start(bf16[4,2,6144]{2,1,0:T(2,128)(2,1)} %reshape.167), calls=%async_computation.2 | async-start | bytes 196608 | tf_op jit(solution)/shard_map/all_to_all | solution.py:106
  26.3 1.0 %copy-start.1 = (bf16[1,1,64,768]{3,2,1,0:T(8,128)(2,1)S(1)}, bf16[1,1,64,768]{3,2,1,0:T(8,128)(2,1)}, u32[]{:S(2)}) copy-start(bf16[1,1,64,768]{3,2,1,0:T(8,128)(2,1)} %param.10) | copy-start | bytes 294916
  44.2 1.0 %copy-start.3 = (bf16[1,1,64,768]{3,2,1,0:T(8,128)(2,1)S(1)}, bf16[1,1,64,768]{3,2,1,0:T(8,128)(2,1)}, u32[]{:S(2)}) copy-start(bf16[1,1,64,768]{3,2,1,0:T(8,128)(2,1)} %param.9) | copy-start | bytes 294916
  46.4 0.9 %copy-start.2 = (bf16[1,1,64,768]{3,2,1,0:T(8,128)(2,1)S(1)}, bf16[1,1,64,768]{3,2,1,0:T(8,128)(2,1)}, u32[]{:S(2)}) copy-start(bf16[1,1,64,768]{3,2,1,0:T(8,128)(2,1)} %param.12) | copy-start | bytes 294916
  46.4 0.9 %copy-start.4 = (bf16[1,1,64,768]{3,2,1,0:T(8,128)(2,1)S(1)}, bf16[1,1,64,768]{3,2,1,0:T(8,128)(2,1)}, u32[]{:S(2)}) copy-start(bf16[1,1,64,768]{3,2,1,0:T(8,128)(2,1)} %param.8) | copy-start | bytes 294916
  47.3 14.5 %copy-start = (bf16[1,1,64,768]{3,2,1,0:T(8,128)(2,1)}, bf16[1,1,64,768]{3,2,1,0:T(8,128)(2,1)S(1)}, u32[]{:S(2)}) copy-start(bf16[1,1,64,768]{3,2,1,0:T(8,128)(2,1)S(1)} %convert_element_type.89) | copy-start | bytes 294916
  50.1 7.7 %all-to-all-start = ((bf16[4,2,6144]{2,1,0:T(2,128)(2,1)}), bf16[4,2,6144]{2,1,0:T(2,128)(2,1)S(1)}, u32[]{:S(2)}, u32[]{:S(2)}) async-start(bf16[4,2,6144]{2,1,0:T(2,128)(2,1)} %reshape.169), calls=%async_computation | async-start | bytes 196608 | tf_op jit(solution)/shard_map/all_to_all | solution.py:107
  57.8 7.1 %all-to-all-start.1 = ((bf16[4,1,1,16,768]{4,3,2,1,0:T(8,128)(2,1)}), bf16[4,1,1,16,768]{4,3,2,1,0:T(8,128)(2,1)S(1)}, u32[]{:S(2)}, u32[]{:S(2)}) async-start(bf16[4,1,1,16,768]{4,3,2,1,0:T(8,128)(2,1)} %pad_maximum_fusion), calls=%async_computation.1 | async-start | bytes 196608 | tf_op jit(solution)/shard_map/all_to_all | solution.py:101
  65.9 16.5 %copy-start.5 = (f32[3,3,768]{2,1,0:T(4,128)S(1)}, f32[3,3,768]{2,1,0:T(4,128)}, u32[]{:S(2)}) copy-start(f32[3,3,768]{2,1,0:T(4,128)} %param.14) | copy-start | bytes 82948
  66.4 17.7 %copy-start.6 = (f32[768]{0:T(1024)S(1)}, f32[768]{0:T(1024)}, u32[]{:S(2)}) copy-start(f32[768]{0:T(1024)} %param.15) | copy-start | bytes 9220
  72.9 9.9 %collective-permute-start.1 = (bf16[1,1,64,768]{3,2,1,0:T(8,128)(2,1)S(1)}, bf16[1,1,64,768]{3,2,1,0:T(8,128)(2,1)S(1)}, u32[]{:S(2)}, u32[]{:S(2)}) collective-permute-start(bf16[1,1,64,768]{3,2,1,0:T(8,128)(2,1)S(1)} %fusion.38), channel_id=1, source_target_pairs={{1,0},{2,1},{3,2},{4,3},{5,4},{6,5},{7,6},{9,8},{10,9},{11,10},{12... | collective-permute-start | bytes 294920 | tf_op jit(solution)/shard_map/ppermute | solution.py:19
  78.6 5.4 %collective-permute-start = (bf16[1,1,64,768]{3,2,1,0:T(8,128)(2,1)S(1)}, bf16[1,1,64,768]{3,2,1,0:T(8,128)(2,1)S(1)}, u32[]{:S(2)}, u32[]{:S(2)}) collective-permute-start(bf16[1,1,64,768]{3,2,1,0:T(8,128)(2,1)S(1)} %fusion.38), channel_id=1, source_target_pairs={{0,1},{1,2},{2,3},{3,4},{4,5},{5,6},{6,7},{8,9},{9,10},{10,11},{11... | collective-permute-start | bytes 294920 | tf_op jit(solution)/shard_map/ppermute | solution.py:16
